TPU v7x, 256 devices: a whole 4x4x8 slice. The times are simulated.
256 devices in a mesh: row: 8 (over x, y_lo), col: 32 (over z, y_hi, core).
Axes of the slice: x: 4, y: 4 (y_hi: 2, y_lo: 2; y = y_hi * 2 + y_lo), z: 8, core: 2. Of those that a mesh axis runs over, the one named last changes fastest.
Arguments:
- covariance: float32 [12288, 12288], P('row', 'col'), may hold values from -25 to 25, as said below
- process_noise: float32 [12288, 12288], P('row', 'col'), may hold values from -3 to 3, as said below
- wind_heading: int32 [12288], replicated, may hold values from 0 to 7
- wind_speed: int32 [12288], replicated, may hold values from 0 to 7
- mixing_index: int32 [12288], replicated, may hold values from 0 to 7
Outputs:
- forecast: float32 [12288, 12288], P('row', 'col')
Inputs may be any that keep to these rules, and one draw needn't show every extreme that they name: `covariance`: symmetric. `process_noise`: symmetric.
All inputs are finite; a program needn't handle non-finite values.
Results may differ from a plain program's by a relative error of at most 0.00002.
Values sent between devices are 32-bit elements; how exact they have to be, the bound alone decides.
No kernel may reach another device: no remote copies, remote signals or barrier semaphores. Data moves between devices by JAX's collectives and lax.ppermute only.
A program may use at most 64 MiB of HBM per device.

v0:
```python
import functools

import jax
import jax.numpy as jnp
from jax import lax
from jax.experimental import pallas as pl
from jax.experimental.pallas import tpu as pltpu
from jax.sharding import PartitionSpec as P

GY = 96
STEPS = 4
HALO = STEPS * GY
LANES = 128
KINDS = 6
COL = 32
PAD = 8


def find_flows(codes, flows):
    heading, speed, mixing = [code[...] for code in codes]
    tiles = heading.shape[0]
    rate = 0.1 + 0.075 * speed.astype(jnp.float32)
    diagonal = heading % 2 == 1
    length = jnp.where(diagonal, 0.5**0.5, 1.0).astype(jnp.float32)
    cosine = jnp.where((heading == 2) | (heading == 6), 0.0, length)
    cosine = jnp.where((heading > 2) & (heading < 6), -cosine, cosine)
    sine = jnp.where((heading == 0) | (heading == 4), 0.0, length)
    sine = jnp.where(heading > 4, -sine, sine)
    flows[...] = jnp.zeros_like(flows)
    inside = pl.ds(PAD, tiles)
    flows[0, inside, :] = rate * cosine
    flows[1, inside, :] = rate * sine
    flows[2, inside, :] = 0.02 + 0.02 * mixing.astype(jnp.float32)


def line(index):
    return pl.ds(pl.multiple_of(index * GY, GY), GY)


def widen(flows, first, lines, wide, at):
    zero = jnp.zeros((1, LANES), jnp.float32)

    def one(t, _):
        for tile in (3 * t, 3 * t + 1, 3 * t + 2):
            lanes = [flows[k, pl.ds(PAD + first + tile, 1), :] for k in range(3)]
            part = jnp.concatenate(lanes + [jnp.zeros((5, LANES), jnp.float32)], axis=0).T
            east, north, mixing = [jnp.broadcast_to(part[:, k : k + 1], (LANES, LANES)) for k in range(3)]
            west_part, east_part = jnp.maximum(east, 0.0) + mixing, jnp.maximum(-east, 0.0) + mixing
            south_part, north_part = jnp.maximum(north, 0.0) + mixing, jnp.maximum(-north, 0.0) + mixing
            spot = pl.ds(pl.multiple_of(tile * LANES + at, 8), LANES)
            wide[0, spot, :] = 1.0 - west_part - east_part
            wide[1, spot, :] = west_part
            wide[2, spot, :] = east_part
            wide[3, spot, :] = 1.0 - south_part - north_part
            wide[4, spot, :] = south_part
            wide[5, spot, :] = north_part
        for g in range(4):
            edge = pl.multiple_of((4 * t + g) * GY + at, 8)
            wide[4, pl.ds(edge, 1), :] = zero
            wide[5, pl.ds(edge + GY - 1, 1), :] = zero
        return 0

    lax.fori_loop(0, lines // 4, one, 0)


def line_step(rows, wide, at, store, tiles):
    w = [wide[kind, line(at), :] for kind in range(KINDS)]
    for tile in range(tiles):
        lower, middle, upper = [
            ref[line(number), pl.ds(skip + tile * LANES, LANES)] for ref, number, skip in rows
        ]
        along = w[0] * middle + w[1] * lower + w[2] * upper
        store(
            slice(tile * LANES, (tile + 1) * LANES),
            w[3] * along + w[4] * pltpu.roll(along, 1, 0) + w[5] * pltpu.roll(along, GY - 1, 0),
        )


def step(source, shift, target, to, wide, at, count, skip=0):
    def one(pair, _):
        for g in (2 * pair, 2 * pair + 1):

            def store(lanes, value):
                target[line(to + g), lanes] = value

            line_step(
                [(source, shift + g + k, skip) for k in range(3)], wide, at + g, store, target.shape[1] // LANES
            )
        return 0

    lax.fori_loop(0, count // 2, one, 0)


def cut_kernel(pieces, spots, field, *refs):
    outs, sems = refs[: len(pieces)], refs[len(pieces)]
    odd = spots[0] // COL % 2
    for number, (row, lane) in enumerate(pieces):
        out = outs[number]
        rows, lanes = out.shape

        def copy(start):
            part = field.at[pl.ds(start, rows), pl.ds(lane, lanes)]
            return pltpu.make_async_copy(part, out, sems.at[number])

        if row in ("outer", "inner"):
            side = odd if row == "outer" else 1 - odd
            copy(pl.multiple_of(side * (field.shape[0] - rows), 8)).start()
        else:
            copy(row).start()
    for number, (row, lane) in enumerate(pieces):
        out = outs[number]
        part = field.at[pl.ds(0, out.shape[0]), pl.ds(lane, out.shape[1])]
        pltpu.make_async_copy(part, out, sems.at[number]).wait()


def weights_kernel(lines, spots, *refs):
    codes, (wide, flows) = refs[:3], refs[3:]
    find_flows(codes, flows)
    pair = spots[0] // COL // 2
    widen(flows, pair * (2 * lines * GY // LANES) - HALO // LANES, 2 * lines + 2 * STEPS, wide, 0)


def block_kernel(mode, lane, spots, wide, far, field, other, out, *refs):
    full, odd, even = refs[-3:]
    rows = field.shape[0]
    lines = rows // GY
    lanes = slice(lane, lane + LANES)
    index = spots[0] // COL
    upper, lower, every = slice(0, HALO), slice(rows - HALO, rows), slice(0, LANES)
    full[HALO : HALO + rows, :] = other[...] if mode == "passed" else field[:, lanes]
    if mode == "own":
        full[:HALO, :] = far[...]
        full[HALO + rows :, :] = other[...]
    else:
        block = index + 1 if mode == "passed" else index
        next_ref, next_lanes = (field, lanes) if mode == "passed" else (other, every)
        far_lanes = lanes if mode == "passed" else every

        @pl.when(block % 2 == 0)
        def _():
            full[:HALO, :] = far[:, far_lanes]
            full[HALO + rows :, :] = next_ref[upper, next_lanes]
            if mode == "passed":
                refs[0][...] = other[upper, :]

        @pl.when(block % 2 == 1)
        def _():
            full[:HALO, :] = next_ref[lower, next_lanes]
            full[HALO + rows :, :] = far[:, far_lanes]
            if mode == "passed":
                refs[0][...] = other[lower, :]

    at = ((index + 1 if mode == "passed" else index) % 2) * lines
    step(full, 0, odd, 0, wide, at + 1, lines + 6)
    step(odd, 0, even, 0, wide, at + 2, lines + 4)
    step(even, 0, odd, 0, wide, at + 3, lines + 2)
    step(odd, 0, out, 0, wide, at + 4, lines)


def adjoint_kernel(spots, *refs):
    codes, (out_high, out_low, flows, wide, held, field) = refs[:3], refs[3:]
    cols = field.shape[1]
    tiles = [slice(tile * LANES, (tile + 1) * LANES) for tile in range(cols // LANES)]
    lines = 3 * STEPS
    find_flows(codes, flows)
    widen(flows, (spots[0] % COL - 1) * (HALO // LANES), lines, wide, GY)
    zero = jnp.zeros((GY, LANES), jnp.float32)
    for kind in range(KINDS):
        wide[kind, :GY, :] = zero
        wide[kind, GY + lines * GY :, :] = zero
    held[...] = jnp.zeros_like(held)
    place = lax.broadcasted_iota(jnp.int32, (HALO, cols), 0)
    lane = lax.broadcasted_iota(jnp.int32, (HALO, cols), 1)
    field[HALO : 2 * HALO, :] = jnp.where(place == lane, 1.0, 0.0).astype(jnp.float32)
    for number in range(STEPS):
        low, high = STEPS - number, 2 * STEPS + number

        def across(pair, _):
            for g in (2 * pair, 2 * pair + 1):
                w = [wide[kind, line(low + g + 1), :] for kind in (3, 4, 5)]
                for lanes in tiles:
                    here = field[line(low + g), lanes]
                    held[line(low + g + 1), lanes] = (
                        w[0] * here + pltpu.roll(w[1] * here, GY - 1, 0) + pltpu.roll(w[2] * here, 1, 0)
                    )
            return 0

        def along(pair, _):
            for g in (2 * pair, 2 * pair + 1):
                w = [wide[kind, line(low + g + at), :] for kind, at in ((0, 0), (1, 1), (2, -1))]
                for lanes in tiles:
                    new = (
                        w[0] * held[line(low + g), lanes]
                        + w[1] * held[line(low + g + 1), lanes]
                        + w[2] * held[line(low + g - 1), lanes]
                    )
                    if number == STEPS - 1:
                        high_part = new.astype(jnp.bfloat16)
                        out_high[line(low + g - 1), lanes] = high_part
                        out_low[line(low + g - 1), lanes] = (new - high_part.astype(jnp.float32)).astype(
                            jnp.bfloat16
                        )
                    else:
                        field[line(low + g - 1), lanes] = new
            return 0

        lax.fori_loop(0, (high - low) // 2, across, 0)
        lax.fori_loop(0, (high - low + 2) // 2, along, 0)


def product_kernel(terms, spots, *refs):
    count = len(terms)
    fields, (spread_high, spread_low, base) = refs[:count], refs[count : count + 3]
    out, held = refs[-2:]

    @pl.when(pl.program_id(0) == 0)
    def _():
        off = 2 * (spots[0] % 2)
        for number, (kind, lane) in enumerate(terms):
            index = {"own": 1, "on": 2 - off, "off": off}[kind]
            part = pl.ds(pl.multiple_of(index * HALO + lane, LANES), LANES)
            for at, spread in enumerate((spread_high, spread_high, spread_low)):
                first = (at * count + number) * LANES
                held[first : first + LANES, :] = spread[part, :]

    rows = pl.ds(pl.multiple_of(pl.program_id(0) * SUB, SUB), SUB)
    values = [field[rows, :] for field in fields]
    high = [value.astype(jnp.bfloat16) for value in values]
    low = [(value - part.astype(jnp.float32)).astype(jnp.bfloat16) for value, part in zip(values, high)]
    into = rows if out.shape[0] > SUB else slice(None)
    out[into, :] = base[rows, :] + jnp.dot(
        jnp.concatenate(high + low + high, axis=1), held[...], preferred_element_type=jnp.float32
    )


def cost(flops, moved):
    return pl.CostEstimate(flops=flops, bytes_accessed=moved, transcendentals=0)


def shape(*dims):
    return jax.ShapeDtypeStruct(dims, jnp.float32)


def scratch(*dims):
    return pltpu.VMEM(dims, jnp.float32)


def shifted(block, axis, pairs):
    count = lax.axis_size(axis)
    return lax.ppermute(block, axis, [(i, j) for i, j in map(pairs, range(count)) if 0 <= j < count])


HERE = pl.BlockSpec(memory_space=pltpu.VMEM)
SCALARS = pl.BlockSpec(memory_space=pltpu.SMEM)
SUB = 384
ROOM = pltpu.CompilerParams(vmem_limit_bytes=14 << 20)


WIDE_ROOM = pltpu.CompilerParams(vmem_limit_bytes=18 << 20)


def near(array):
    return pltpu.with_memory_space_constraint(array, pltpu.VMEM)


def body(covariance, process_noise, wind_heading, wind_speed, mixing_index):
    rows, cols = covariance.shape
    lines = rows // GY
    codes = [code.reshape(-1, LANES) for code in (wind_heading, wind_speed, mixing_index)]
    place = lax.axis_index("row") * lax.axis_size("col") + lax.axis_index("col")
    spots = place.astype(jnp.int32).reshape(1)
    flow_room = scratch(3, 2 * PAD + codes[0].shape[0], LANES)
    on_pairs = lambda i: (i, i ^ 1)
    off_pairs = lambda i: (i, i + 1 if i % 2 else i - 1)

    def relay_off_pairs():
        count = lax.axis_size("col")
        pairs = [off_pairs(i) for i in range(count)]
        return [
            (r * count + i, (r ^ 1) * count + j)
            for r in range(lax.axis_size("row"))
            for i, j in pairs
            if 0 <= j < count
        ]

    def cut(source, pieces, shapes, space):
        return pl.pallas_call(
            functools.partial(cut_kernel, pieces),
            in_specs=[SCALARS, pl.BlockSpec(memory_space=space)],
            out_specs=[HERE] * len(pieces),
            out_shape=[shape(*dims) for dims in shapes],
            scratch_shapes=[pltpu.SemaphoreType.DMA((len(pieces),))],
            cost_estimate=cost(0, 1 << 22),
            compiler_params=ROOM,
        )(spots, source)

    chunks = range(0, cols, LANES)
    late = chunks[-1]
    hbm = pltpu.HBM
    raw_0, raw_late, edge = cut(
        covariance, [(0, 0), (0, late), ("outer", 0)], [(rows, LANES), (rows, LANES), (HALO, late)], hbm
    )
    swap = lambda piece: shifted(piece, "row", lambda i: (i, i ^ 1))
    x_out = lambda i: (i, i + 2 if i % 2 else i - 2)
    x_in = lambda i: (i, i - 2 if i % 2 else i + 2)
    swapped = [swap(raw_0)]
    crossed = lax.ppermute(raw_late, ("row", "col"), relay_off_pairs())
    far_other = shifted(edge, "row", x_out)
    raw_1, above, below = cut(
        covariance, [(0, LANES), (rows - HALO, late), (0, late)], [(rows, LANES), (HALO, LANES), (HALO, LANES)], hbm
    )
    swapped.append(swap(raw_1))
    above = shifted(above, "row", lambda i: (i, i + 1))
    below = shifted(below, "row", lambda i: (i, i - 1))
    near_field = near(covariance)
    spread = pl.pallas_call(
        adjoint_kernel,
        in_specs=[SCALARS, HERE, HERE, HERE],
        out_specs=[HERE, HERE],
        out_shape=[jax.ShapeDtypeStruct((3 * HALO, cols), jnp.bfloat16)] * 2,
        scratch_shapes=[
            flow_room,
            scratch(KINDS, 3 * HALO + 2 * GY, LANES),
            scratch(3 * HALO + 2 * GY, cols),
            scratch(3 * HALO, cols),
        ],
        cost_estimate=cost(2 * 6 * 4 * 3 * HALO * cols, 4 * 3 * HALO * cols),
        compiler_params=ROOM,
        name="spread",
    )(spots, *codes)
    spread = [near(part) for part in spread]
    long = rows + 2 * HALO
    wide = pl.pallas_call(
        functools.partial(weights_kernel, lines),
        in_specs=[SCALARS] + [HERE] * 3,
        out_specs=HERE,
        out_shape=shape(KINDS, rows + long, LANES),
        scratch_shapes=[flow_room],
        cost_estimate=cost(0, 1 << 24),
        compiler_params=WIDE_ROOM,
        name="weights",
    )(spots, *codes)

    def block_part(mode, lane, far, field, other):
        outs = [shape(rows, LANES)] + ([shape(HALO, LANES)] if mode == "passed" else [])
        return pl.pallas_call(
            functools.partial(block_kernel, mode, lane),
            in_specs=[SCALARS] + [HERE] * 4,
            out_specs=[HERE] * len(outs),
            out_shape=outs,
            scratch_shapes=[scratch(long, LANES)] * 3,
            cost_estimate=cost(6 * 4 * rows * cols, 4 * rows * cols),
            compiler_params=ROOM,
        )(spots, near(wide), near(far), near(field), near(other))

    def call(terms, base, final=False):
        width = LANES * len(terms)
        moved = 4 * rows * (width + 2 * cols)
        return pl.pallas_call(
            functools.partial(product_kernel, [(kind, lane) for _, kind, lane in terms]),
            grid=(rows // SUB,),
            in_specs=[SCALARS] + [HERE] * (len(terms) + 3),
            out_specs=pl.BlockSpec((SUB, cols), lambda i: (i, 0)) if final else HERE,
            out_shape=shape(rows, cols),
            scratch_shapes=[pltpu.VMEM((3 * width, cols), jnp.bfloat16)],
            cost_estimate=cost(6 * rows * cols * width, moved),
            compiler_params=ROOM,
        )(spots, *[near(field) for field, _, _ in terms], *spread, near(base))

    kept, kept_on, relayed = [], [], []
    for number, other in enumerate(swapped):
        lane = chunks[number]
        passed, back = block_part("passed", lane, far_other, near_field, other)
        relayed.append(lax.ppermute(passed, ("row", "col"), relay_off_pairs()))
        far_mine = shifted(back, "row", x_in)
        kept += block_part("kept", lane, far_mine, near_field, other)
        kept_on.append(shifted(kept[-1], "col", on_pairs))
    turned = swap(crossed)
    (crossed_edge,) = cut(crossed, [("inner", 0)], [(HALO, LANES)], pl.ANY)
    far_off = shifted(crossed_edge, "row", x_in)
    kept += block_part("own", late, above, near_field, below)
    kept_on.append(shifted(kept[-1], "col", on_pairs))
    relayed += block_part("off", 0, far_off, turned, crossed)

    def near_terms(number):
        lane = chunks[number]
        return [(kept[number], "own", lane), (kept_on[number], "on", lane)]

    def far_terms(number):
        return [(relayed[number], "off", chunks[number])]

    result = call(near_terms(0), process_noise)
    result = call(near_terms(1) + far_terms(0), result)
    return call(near_terms(2) + far_terms(1) + far_terms(2), result, True)


def solution(mesh):
    return jax.shard_map(
        body,
        mesh=mesh,
        in_specs=(P("row", "col"), P("row", "col"), P(), P(), P()),
        out_specs=P("row", "col"),
        check_vma=False,
    )
```

profile of v0, /device:TPU:35, one launch (start us, length us, event | category | flops | bytes accessed | tf_op | source)
XLA Modules:
  0.0 110.3 jit_solution(7720108561420573191)
XLA Ops:
  0.0 0.0 copy-start
  0.0 1.7 %copy-done = f32[1536,384]{1,0:T(8,128)S(1)} copy-done((f32[1536,384]{1,0:T(8,128)S(1)}, f32[1536,384]{1,0:T(8,128)}, u32[]{:S(2)}) %copy-start) | copy-done | bytes 2359320
  1.7 0.0 copy-start.3
  1.7 0.0 copy-start.4
  1.7 0.0 copy-start.5
  1.7 0.2 shard_map.57
  1.8 5.2 %collective-permute-start.6 = (f32[1536,128]{1,0:T(8,128)S(1)}, f32[1536,128]{1,0:T(8,128)S(1)}, u32[]{:S(2)}, u32[]{:S(2)}) collective-permute-start(f32[1536,128]{1,0:T(8,128)S(1)} %get-tuple-element.22), channel_id=1, source_target_pairs={{1,34},{2,33},{3,36},{4,35},{5,38},{6,37},{7,40},{8,39},{9,42},{10... | collective-permute-start | bytes 2359304 | tf_op jit(solution)/shard_map/ppermute | solution.py:307
  7.1 0.1 collective-permute-start.11
  7.2 0.1 shard_map.55
  7.3 1.5 %collective-permute-start.4 = (f32[1536,128]{1,0:T(8,128)S(1)}, f32[1536,128]{1,0:T(8,128)S(1)}, u32[]{:S(2)}, u32[]{:S(2)}) collective-permute-start(f32[1536,128]{1,0:T(8,128)S(1)} %get-tuple-element.20), channel_id=1, source_target_pairs={{0,32},{32,0},{64,96},{96,64},{128,160},{160,128},{192,224},{224,1... | collective-permute-start | bytes 2359304 | tf_op jit(solution)/shard_map/ppermute | solution.py:250
  8.8 2.2 %collective-permute-start.3 = (f32[384,256]{1,0:T(8,128)S(1)}, f32[384,256]{1,0:T(8,128)S(1)}, u32[]{:S(2)}, u32[]{:S(2)}) collective-permute-start(f32[384,256]{1,0:T(8,128)S(1)} %get-tuple-element.19), channel_id=1, source_target_pairs={{32,96},{64,0},{96,160},{128,64},{160,224},{192,128},{33,97},{65,1... | collective-permute-start | bytes 1179656 | tf_op jit(solution)/shard_map/ppermute | solution.py:250
  11.0 14.2 %collective-permute-done.6.field.other = f32[1536,128]{1,0:T(8,128)S(1)} collective-permute-done((f32[1536,128]{1,0:T(8,128)S(1)}, f32[1536,128]{1,0:T(8,128)S(1)}, u32[]{:S(2)}, u32[]{:S(2)}) %collective-permute-start.6) | collective-permute-done | bytes 786464 | tf_op jit(solution)/shard_map/ppermute | solution.py:307
  25.1 0.2 collective-permute-start.8
  25.3 0.0 copy-done.3
  25.3 0.0 copy-done.4
  25.3 0.0 copy-done.5
  25.3 0.0 copy-start.1
  25.3 4.5 %weights.1.wide = f32[6,3840,128]{2,1,0:T(8,128)S(1)} custom-call(s32[1]{0:T(128)} %bitcast.spots, s32[96,128]{1,0:T(8,128)S(1)} %bitcast.4, s32[96,128]{1,0:T(8,128)S(1)} %bitcast.6, s32[96,128]{1,0:T(8,128)S(1)} %bitcast.8), custom_call_target="tpu_custom_call" | custom-call | bytes 16777216 | tf_op jit(solution)/shard_map/weights/pallas_call | solution.py:333
  29.9 0.0 collective-permute-done.3.far
  29.9 0.0 collective-permute-done.11.other
  29.9 0.0 copy-done.1
  29.9 2.3 %shard_map.62 = (f32[1536,128]{1,0:T(8,128)S(1)}, f32[384,128]{1,0:T(8,128)S(1)}) custom-call(s32[1]{0:T(128)} %bitcast.spots, f32[6,3840,128]{2,1,0:T(8,128)S(1)} %weights.1.wide, f32[384,256]{1,0:T(8,128)S(1)} %collective-permute-done.3.far, f32[1536,384]{1,0:T(8,128)S(1)} %copy-done.1, f32[1536,128]{1,0:T(8,128)S(1)} %collective-permute-done.11.other), custom_call_target="tpu_custom_call" | custom-call | flops 14155776 | bytes 2359296 | tf_op jit(solution)/shard_map/pallas_call | solution.py:346
  32.2 3.1 %collective-permute-start.13 = (f32[384,128]{1,0:T(8,128)S(1)}, f32[384,128]{1,0:T(8,128)S(1)}, u32[]{:S(2)}, u32[]{:S(2)}) collective-permute-start(f32[384,128]{1,0:T(8,128)S(1)} %get-tuple-element.28), channel_id=1, source_target_pairs={{0,64},{64,128},{96,32},{128,192},{160,96},{224,160},{1,65},{65,12... | collective-permute-start | bytes 589832 | tf_op jit(solution)/shard_map/ppermute | solution.py:250
  35.3 8.2 %collective-permute-done.4.other = f32[1536,128]{1,0:T(8,128)S(1)} collective-permute-done((f32[1536,128]{1,0:T(8,128)S(1)}, f32[1536,128]{1,0:T(8,128)S(1)}, u32[]{:S(2)}, u32[]{:S(2)}) %collective-permute-start.4) | collective-permute-done | bytes 786464 | tf_op jit(solution)/shard_map/ppermute | solution.py:250
  43.6 2.3 %shard_map.58 = (f32[1536,128]{1,0:T(8,128)S(1)}, f32[384,128]{1,0:T(8,128)S(1)}) custom-call(s32[1]{0:T(128)} %bitcast.spots, f32[6,3840,128]{2,1,0:T(8,128)S(1)} %weights.1.wide, f32[384,256]{1,0:T(8,128)S(1)} %collective-permute-done.3.far, f32[1536,384]{1,0:T(8,128)S(1)} %copy-done.1, f32[1536,128]{1,0:T(8,128)S(1)} %collective-permute-done.4.other), custom_call_target="tpu_custom_call" | custom-call | flops 14155776 | bytes 2359296 | tf_op jit(solution)/shard_map/pallas_call | solution.py:346
  45.8 3.1 %collective-permute-start.9 = (f32[384,128]{1,0:T(8,128)S(1)}, f32[384,128]{1,0:T(8,128)S(1)}, u32[]{:S(2)}, u32[]{:S(2)}) collective-permute-start(f32[384,128]{1,0:T(8,128)S(1)} %get-tuple-element.25), channel_id=1, source_target_pairs={{0,64},{64,128},{96,32},{128,192},{160,96},{224,160},{1,65},{65,12... | collective-permute-start | bytes 589832 | tf_op jit(solution)/shard_map/ppermute | solution.py:250
  49.0 1.9 %collective-permute-start = (f32[384,128]{1,0:T(8,128)S(1)}, f32[384,128]{1,0:T(8,128)S(1)}, u32[]{:S(2)}, u32[]{:S(2)}) collective-permute-start(f32[384,128]{1,0:T(8,128)S(1)} %get-tuple-element.17), channel_id=1, source_target_pairs={{0,32},{32,64},{64,96},{96,128},{128,160},{160,192},{192,224},{1,3... | collective-permute-start | bytes 589832 | tf_op jit(solution)/shard_map/ppermute | solution.py:250
  50.9 4.3 %collective-permute-start.1 = (f32[384,128]{1,0:T(8,128)S(1)}, f32[384,128]{1,0:T(8,128)S(1)}, u32[]{:S(2)}, u32[]{:S(2)}) collective-permute-start(f32[384,128]{1,0:T(8,128)S(1)} %get-tuple-element.18), channel_id=1, source_target_pairs={{32,0},{64,32},{96,64},{128,96},{160,128},{192,160},{224,192},{33,... | collective-permute-start | bytes 589832 | tf_op jit(solution)/shard_map/ppermute | solution.py:250
  55.2 0.0 collective-permute-done.13.far
  55.2 2.3 %shard_map.63.refs_0_ = f32[1536,128]{1,0:T(8,128)S(1)} custom-call(s32[1]{0:T(128)} %bitcast.spots, f32[6,3840,128]{2,1,0:T(8,128)S(1)} %weights.1.wide, f32[384,128]{1,0:T(8,128)S(1)} %collective-permute-done.13.far, f32[1536,384]{1,0:T(8,128)S(1)} %copy-done.1, f32[1536,128]{1,0:T(8,128)S(1)} %collective-permute-done.11.other), custom_call_target="tpu_custom_call" | custom-call | flops 14155776 | bytes 2359296 | tf_op jit(solution)/shard_map/pallas_call | solution.py:346
  57.5 1.0 collective-permute-start.14
  58.5 0.2 shard_map.59
  58.7 0.0 collective-permute-done.9.far
  58.7 2.8 %collective-permute-start.7 = (f32[384,128]{1,0:T(8,128)S(1)}, f32[384,128]{1,0:T(8,128)S(1)}, u32[]{:S(2)}, u32[]{:S(2)}) collective-permute-start(f32[384,128]{1,0:T(8,128)S(1)} %shard_map.59), channel_id=1, source_target_pairs={{0,64},{64,128},{96,32},{128,192},{160,96},{224,160},{1,65},{65,12... | collective-permute-start | bytes 589832 | tf_op jit(solution)/shard_map/ppermute | solution.py:250
  61.6 2.3 %shard_map.61.refs_0_ = f32[1536,128]{1,0:T(8,128)S(1)} custom-call(s32[1]{0:T(128)} %bitcast.spots, f32[6,3840,128]{2,1,0:T(8,128)S(1)} %weights.1.wide, f32[384,128]{1,0:T(8,128)S(1)} %collective-permute-done.9.far, f32[1536,384]{1,0:T(8,128)S(1)} %copy-done.1, f32[1536,128]{1,0:T(8,128)S(1)} %collective-permute-done.4.other), custom_call_target="tpu_custom_call" | custom-call | flops 14155776 | bytes 2359296 | tf_op jit(solution)/shard_map/pallas_call | solution.py:346
  63.9 2.5 %collective-permute-done.far = f32[384,128]{1,0:T(8,128)S(1)} collective-permute-done((f32[384,128]{1,0:T(8,128)S(1)}, f32[384,128]{1,0:T(8,128)S(1)}, u32[]{:S(2)}, u32[]{:S(2)}) %collective-permute-start) | collective-permute-done | bytes 196640 | tf_op jit(solution)/shard_map/ppermute | solution.py:250
  66.3 4.6 %collective-permute-start.12 = (f32[1536,128]{1,0:T(8,128)S(1)}, f32[1536,128]{1,0:T(8,128)S(1)}, u32[]{:S(2)}, u32[]{:S(2)}) collective-permute-start(f32[1536,128]{1,0:T(8,128)S(1)} %get-tuple-element.27), channel_id=1, source_target_pairs={{1,34},{2,33},{3,36},{4,35},{5,38},{6,37},{7,40},{8,39},{9,42},{10... | collective-permute-start | bytes 2359304 | tf_op jit(solution)/shard_map/ppermute | solution.py:374
  70.9 0.0 collective-permute-done.1.other
  70.9 0.2 collective-permute-start.10
  71.1 2.3 %shard_map.56.refs_0_ = f32[1536,128]{1,0:T(8,128)S(1)} custom-call(s32[1]{0:T(128)} %bitcast.spots, f32[6,3840,128]{2,1,0:T(8,128)S(1)} %weights.1.wide, f32[384,128]{1,0:T(8,128)S(1)} %collective-permute-done.far, f32[1536,384]{1,0:T(8,128)S(1)} %copy-done.1, f32[384,128]{1,0:T(8,128)S(1)} %collective-permute-done.1.other), custom_call_target="tpu_custom_call" | custom-call | flops 14155776 | bytes 2359296 | tf_op jit(solution)/shard_map/pallas_call | solution.py:346
  73.4 0.0 collective-permute-done.7.far
  73.4 0.5 collective-permute-start.2
  73.9 0.0 collective-permute-done.8.field
  73.9 3.2 %collective-permute-start.5 = (f32[1536,128]{1,0:T(8,128)S(1)}, f32[1536,128]{1,0:T(8,128)S(1)}, u32[]{:S(2)}, u32[]{:S(2)}) collective-permute-start(f32[1536,128]{1,0:T(8,128)S(1)} %get-tuple-element.21), channel_id=1, source_target_pairs={{1,34},{2,33},{3,36},{4,35},{5,38},{6,37},{7,40},{8,39},{9,42},{10... | collective-permute-start | bytes 2359304 | tf_op jit(solution)/shard_map/ppermute | solution.py:374
  77.0 4.3 %spread.1 = (bf16[1152,384]{1,0:T(8,128)(2,1)S(1)}, bf16[1152,384]{1,0:T(8,128)(2,1)S(1)}) custom-call(s32[1]{0:T(128)} %bitcast.spots, s32[96,128]{1,0:T(8,128)S(1)} %bitcast.5, s32[96,128]{1,0:T(8,128)S(1)} %bitcast.7, s32[96,128]{1,0:T(8,128)S(1)} %bitcast.9), custom_call_target="tpu_custom_call" | custom-call | flops 21233664 | bytes 1769472 | tf_op jit(solution)/shard_map/spread/pallas_call | solution.py:316
  81.3 0.0 copy-start.2
  81.3 2.3 %shard_map.60.refs_3_ = f32[1536,128]{1,0:T(8,128)S(1)} custom-call(s32[1]{0:T(128)} %bitcast.spots, f32[6,3840,128]{2,1,0:T(8,128)S(1)} %weights.1.wide, f32[384,128]{1,0:T(8,128)S(1)} %collective-permute-done.7.far, f32[1536,128]{1,0:T(8,128)S(1)} %collective-permute-done.8.field, f32[1536,128]{1,0:T(8,128)S(1)} %collective-permute-done.6.field.other), custom_call_target="tpu_custom_call" | custom-call | flops 14155776 | bytes 2359296 | tf_op jit(solution)/shard_map/pallas_call | solution.py:346
  83.6 0.0 collective-permute-done.14.refs_1_
  83.6 0.0 copy-done.2
  83.7 2.1 %shard_map.64.refs_5_ = f32[1536,384]{1,0:T(8,128)S(1)} custom-call(s32[1]{0:T(128)} %bitcast.spots, f32[1536,128]{1,0:T(8,128)S(1)} %shard_map.63.refs_0_, f32[1536,128]{1,0:T(8,128)S(1)} %collective-permute-done.14.refs_1_, bf16[1152,384]{1,0:T(8,128)(2,1)S(1)} %get-tuple-element.23.refs_2_.refs_3_.refs_4_, ...), custom_call_target="tpu_custom_call" | custom-call | flops 905969664 | bytes 6291456 | tf_op jit(solution)/shard_map/pallas_call | solution.py:359
  85.7 12.0 %collective-permute-done.12.refs_2_ = f32[1536,128]{1,0:T(8,128)S(1)} collective-permute-done((f32[1536,128]{1,0:T(8,128)S(1)}, f32[1536,128]{1,0:T(8,128)S(1)}, u32[]{:S(2)}, u32[]{:S(2)}) %collective-permute-start.12) | collective-permute-done | bytes 786464 | tf_op jit(solution)/shard_map/ppermute | solution.py:374
  97.7 0.0 collective-permute-done.10.refs_1_
  97.7 2.7 %shard_map.65.refs_6_ = f32[1536,384]{1,0:T(8,128)S(1)} custom-call(s32[1]{0:T(128)} %bitcast.spots, f32[1536,128]{1,0:T(8,128)S(1)} %shard_map.61.refs_0_, f32[1536,128]{1,0:T(8,128)S(1)} %collective-permute-done.10.refs_1_, f32[1536,128]{1,0:T(8,128)S(1)} %collective-permute-done.12.refs_2_, ...), custom_call_target="tpu_custom_call" | custom-call | flops 1358954496 | bytes 7077888 | tf_op jit(solution)/shard_map/pallas_call | solution.py:359
  100.4 0.0 collective-permute-done.2.refs_1_
  100.4 5.7 %collective-permute-done.5.refs_2_ = f32[1536,128]{1,0:T(8,128)S(1)} collective-permute-done((f32[1536,128]{1,0:T(8,128)S(1)}, f32[1536,128]{1,0:T(8,128)S(1)}, u32[]{:S(2)}, u32[]{:S(2)}) %collective-permute-start.5) | collective-permute-done | bytes 786464 | tf_op jit(solution)/shard_map/ppermute | solution.py:374
  106.1 4.1 %shard_map.66 = f32[1536,384]{1,0:T(8,128)} custom-call(s32[1]{0:T(128)} %bitcast.spots, f32[1536,128]{1,0:T(8,128)S(1)} %shard_map.56.refs_0_, f32[1536,128]{1,0:T(8,128)S(1)} %collective-permute-done.2.refs_1_, f32[1536,128]{1,0:T(8,128)S(1)} %collective-permute-done.5.refs_2_, f32[1536,128]{1,0:T(8,128)S(1)} %shard_map.60.refs_3_, ...), custom_call_target="tpu_custom_call" | custom-call | flops 1811939328 | bytes 7864320 | tf_op jit(solution)/shard_map/pallas_call | solution.py:359
Async XLA Ops:
  0.0 1.7 %copy-start = (f32[1536,384]{1,0:T(8,128)S(1)}, f32[1536,384]{1,0:T(8,128)}, u32[]{:S(2)}) copy-start(f32[1536,384]{1,0:T(8,128)} %field.13) | copy-start | bytes 7077892
  1.7 23.6 %copy-start.3 = (s32[12288]{0:T(1024)S(1)}, s32[12288]{0:T(1024)}, u32[]{:S(2)}) copy-start(s32[12288]{0:T(1024)} %param.7) | copy-start | bytes 147460
  1.7 23.6 %copy-start.4 = (s32[12288]{0:T(1024)S(1)}, s32[12288]{0:T(1024)}, u32[]{:S(2)}) copy-start(s32[12288]{0:T(1024)} %param.8) | copy-start | bytes 147460
  1.7 23.6 %copy-start.5 = (s32[12288]{0:T(1024)S(1)}, s32[12288]{0:T(1024)}, u32[]{:S(2)}) copy-start(s32[12288]{0:T(1024)} %param.9) | copy-start | bytes 147460
  1.8 23.3 %collective-permute-start.6 = (f32[1536,128]{1,0:T(8,128)S(1)}, f32[1536,128]{1,0:T(8,128)S(1)}, u32[]{:S(2)}, u32[]{:S(2)}) collective-permute-start(f32[1536,128]{1,0:T(8,128)S(1)} %get-tuple-element.22), channel_id=1, source_target_pairs={{1,34},{2,33},{3,36},{4,35},{5,38},{6,37},{7,40},{8,39},{9,42},{10... | collective-permute-start | bytes 2359304 | tf_op jit(solution)/shard_map/ppermute | solution.py:307
  7.1 22.8 %collective-permute-start.11 = (f32[1536,128]{1,0:T(8,128)S(1)}, f32[1536,128]{1,0:T(8,128)S(1)}, u32[]{:S(2)}, u32[]{:S(2)}) collective-permute-start(f32[1536,128]{1,0:T(8,128)S(1)} %get-tuple-element.26), channel_id=1, source_target_pairs={{0,32},{32,0},{64,96},{96,64},{128,160},{160,128},{192,224},{224,1... | collective-permute-start | bytes 2359304 | tf_op jit(solution)/shard_map/ppermute | solution.py:250
  7.3 36.3 %collective-permute-start.4 = (f32[1536,128]{1,0:T(8,128)S(1)}, f32[1536,128]{1,0:T(8,128)S(1)}, u32[]{:S(2)}, u32[]{:S(2)}) collective-permute-start(f32[1536,128]{1,0:T(8,128)S(1)} %get-tuple-element.20), channel_id=1, source_target_pairs={{0,32},{32,0},{64,96},{96,64},{128,160},{160,128},{192,224},{224,1... | collective-permute-start | bytes 2359304 | tf_op jit(solution)/shard_map/ppermute | solution.py:250
  8.8 21.0 %collective-permute-start.3 = (f32[384,256]{1,0:T(8,128)S(1)}, f32[384,256]{1,0:T(8,128)S(1)}, u32[]{:S(2)}, u32[]{:S(2)}) collective-permute-start(f32[384,256]{1,0:T(8,128)S(1)} %get-tuple-element.19), channel_id=1, source_target_pairs={{32,96},{64,0},{96,160},{128,64},{160,224},{192,128},{33,97},{65,1... | collective-permute-start | bytes 1179656 | tf_op jit(solution)/shard_map/ppermute | solution.py:250
  25.1 48.7 %collective-permute-start.8 = (f32[1536,128]{1,0:T(8,128)S(1)}, f32[1536,128]{1,0:T(8,128)S(1)}, u32[]{:S(2)}, u32[]{:S(2)}) collective-permute-start(f32[1536,128]{1,0:T(8,128)S(1)} %collective-permute-done.6.field.other), channel_id=1, source_target_pairs={{0,32},{32,0},{64,96},{96,64},{128,160},{160,128},{192,224},{224,1... | collective-permute-start | bytes 2359304 | tf_op jit(solution)/shard_map/ppermute | solution.py:250
  25.3 4.6 %copy-start.1 = (f32[1536,384]{1,0:T(8,128)S(1)}, f32[1536,384]{1,0:T(8,128)}, u32[]{:S(2)}) copy-start(f32[1536,384]{1,0:T(8,128)} %field.13) | copy-start | bytes 7077892
  32.2 23.0 %collective-permute-start.13 = (f32[384,128]{1,0:T(8,128)S(1)}, f32[384,128]{1,0:T(8,128)S(1)}, u32[]{:S(2)}, u32[]{:S(2)}) collective-permute-start(f32[384,128]{1,0:T(8,128)S(1)} %get-tuple-element.28), channel_id=1, source_target_pairs={{0,64},{64,128},{96,32},{128,192},{160,96},{224,160},{1,65},{65,12... | collective-permute-start | bytes 589832 | tf_op jit(solution)/shard_map/ppermute | solution.py:250
  45.8 12.9 %collective-permute-start.9 = (f32[384,128]{1,0:T(8,128)S(1)}, f32[384,128]{1,0:T(8,128)S(1)}, u32[]{:S(2)}, u32[]{:S(2)}) collective-permute-start(f32[384,128]{1,0:T(8,128)S(1)} %get-tuple-element.25), channel_id=1, source_target_pairs={{0,64},{64,128},{96,32},{128,192},{160,96},{224,160},{1,65},{65,12... | collective-permute-start | bytes 589832 | tf_op jit(solution)/shard_map/ppermute | solution.py:250
  49.0 17.4 %collective-permute-start = (f32[384,128]{1,0:T(8,128)S(1)}, f32[384,128]{1,0:T(8,128)S(1)}, u32[]{:S(2)}, u32[]{:S(2)}) collective-permute-start(f32[384,128]{1,0:T(8,128)S(1)} %get-tuple-element.17), channel_id=1, source_target_pairs={{0,32},{32,64},{64,96},{96,128},{128,160},{160,192},{192,224},{1,3... | collective-permute-start | bytes 589832 | tf_op jit(solution)/shard_map/ppermute | solution.py:250
  50.9 20.0 %collective-permute-start.1 = (f32[384,128]{1,0:T(8,128)S(1)}, f32[384,128]{1,0:T(8,128)S(1)}, u32[]{:S(2)}, u32[]{:S(2)}) collective-permute-start(f32[384,128]{1,0:T(8,128)S(1)} %get-tuple-element.18), channel_id=1, source_target_pairs={{32,0},{64,32},{96,64},{128,96},{160,128},{192,160},{224,192},{33,... | collective-permute-start | bytes 589832 | tf_op jit(solution)/shard_map/ppermute | solution.py:250
  57.5 26.2 %collective-permute-start.14 = (f32[1536,128]{1,0:T(8,128)S(1)}, f32[1536,128]{1,0:T(8,128)S(1)}, u32[]{:S(2)}, u32[]{:S(2)}) collective-permute-start(f32[1536,128]{1,0:T(8,128)S(1)} %shard_map.63.refs_0_), channel_id=1, source_target_pairs={{0,1},{1,0},{2,3},{3,2},{4,5},{5,4},{6,7},{7,6},{8,9},{9,8},{10,11... | collective-permute-start | bytes 2359304 | tf_op jit(solution)/shard_map/ppermute | solution.py:250
  58.7 14.6 %collective-permute-start.7 = (f32[384,128]{1,0:T(8,128)S(1)}, f32[384,128]{1,0:T(8,128)S(1)}, u32[]{:S(2)}, u32[]{:S(2)}) collective-permute-start(f32[384,128]{1,0:T(8,128)S(1)} %shard_map.59), channel_id=1, source_target_pairs={{0,64},{64,128},{96,32},{128,192},{160,96},{224,160},{1,65},{65,12... | collective-permute-start | bytes 589832 | tf_op jit(solution)/shard_map/ppermute | solution.py:250
  66.3 31.4 %collective-permute-start.12 = (f32[1536,128]{1,0:T(8,128)S(1)}, f32[1536,128]{1,0:T(8,128)S(1)}, u32[]{:S(2)}, u32[]{:S(2)}) collective-permute-start(f32[1536,128]{1,0:T(8,128)S(1)} %get-tuple-element.27), channel_id=1, source_target_pairs={{1,34},{2,33},{3,36},{4,35},{5,38},{6,37},{7,40},{8,39},{9,42},{10... | collective-permute-start | bytes 2359304 | tf_op jit(solution)/shard_map/ppermute | solution.py:374
  70.9 26.8 %collective-permute-start.10 = (f32[1536,128]{1,0:T(8,128)S(1)}, f32[1536,128]{1,0:T(8,128)S(1)}, u32[]{:S(2)}, u32[]{:S(2)}) collective-permute-start(f32[1536,128]{1,0:T(8,128)S(1)} %shard_map.61.refs_0_), channel_id=1, source_target_pairs={{0,1},{1,0},{2,3},{3,2},{4,5},{5,4},{6,7},{7,6},{8,9},{9,8},{10,11... | collective-permute-start | bytes 2359304 | tf_op jit(solution)/shard_map/ppermute | solution.py:250
  73.4 27.0 %collective-permute-start.2 = (f32[1536,128]{1,0:T(8,128)S(1)}, f32[1536,128]{1,0:T(8,128)S(1)}, u32[]{:S(2)}, u32[]{:S(2)}) collective-permute-start(f32[1536,128]{1,0:T(8,128)S(1)} %shard_map.56.refs_0_), channel_id=1, source_target_pairs={{0,1},{1,0},{2,3},{3,2},{4,5},{5,4},{6,7},{7,6},{8,9},{9,8},{10,11... | collective-permute-start | bytes 2359304 | tf_op jit(solution)/shard_map/ppermute | solution.py:250
  73.9 32.2 %collective-permute-start.5 = (f32[1536,128]{1,0:T(8,128)S(1)}, f32[1536,128]{1,0:T(8,128)S(1)}, u32[]{:S(2)}, u32[]{:S(2)}) collective-permute-start(f32[1536,128]{1,0:T(8,128)S(1)} %get-tuple-element.21), channel_id=1, source_target_pairs={{1,34},{2,33},{3,36},{4,35},{5,38},{6,37},{7,40},{8,39},{9,42},{10... | collective-permute-start | bytes 2359304 | tf_op jit(solution)/shard_map/ppermute | solution.py:374
  81.3 2.3 %copy-start.2 = (f32[1536,384]{1,0:T(8,128)S(1)}, f32[1536,384]{1,0:T(8,128)}, u32[]{:S(2)}) copy-start(f32[1536,384]{1,0:T(8,128)} %refs_4_.1) | copy-start | bytes 7077892
where the time goes:
time: 111 us; the launch traced here: 110 us
  waiting for transfers between devices  42.6 us (38%)
  starting transfers between devices  33.8 us (30%)
  Pallas kernels  31.9 us (29%)
  local copies, waits for them, and re-layouts  1.69 us (2%)
    ppermute x12, starting transfers between devices, shifted(): lax.ppermute(block, axis, [(i, j) for i, j in map(pairs, range(count)) if...  20.9 us
    ppermute x2, waiting for transfers between devices, body(): relayed.append(lax.ppermute(passed, ('row', 'col'), relay_off_pairs()))  17.7 us
    ppermute x1, waiting for transfers between devices, body(): crossed = lax.ppermute(raw_late, ('row', 'col'), relay_off_pairs())  14.2 us
    pallas_call x6, Pallas kernels, block_part(): pl.pallas_call(functools.partial(block_kernel, mode, lane), in_specs=[SCA...  13.7 us
    ppermute x12, waiting for transfers between devices, shifted(): lax.ppermute(block, axis, [(i, j) for i, j in map(pairs, range(count)) if...  10.7 us
    pallas_call x3, Pallas kernels, call(): pl.pallas_call(functools.partial(product_kernel, [(kind, lane) for _, kin...  8.89 us
    ppermute x2, starting transfers between devices, body(): relayed.append(lax.ppermute(passed, ('row', 'col'), relay_off_pairs()))  7.71 us
    ppermute x1, starting transfers between devices, body(): crossed = lax.ppermute(raw_late, ('row', 'col'), relay_off_pairs())  5.2 us
  transfers between devices with their start and end apart: 15, of which 5 were waited for; matrix products, arithmetic and copies ran while one was open for 0% of the time, Pallas kernels for 25%

commit v1 on v0

--- a/solution.py
+++ b/solution.py
@@ -297,9 +297,9 @@
     chunks = range(0, cols, LANES)
     late = chunks[-1]
     hbm = pltpu.HBM
-    raw_0, raw_late, edge = cut(
-        covariance, [(0, 0), (0, late), ("outer", 0)], [(rows, LANES), (rows, LANES), (HALO, late)], hbm
-    )
+    far_field = pltpu.with_memory_space_constraint(covariance, hbm)
+    (raw_0,) = cut(far_field, [(0, 0)], [(rows, LANES)], hbm)
+    raw_late, edge = cut(covariance, [(0, late), ("outer", 0)], [(rows, LANES), (HALO, late)], hbm)
     swap = lambda piece: shifted(piece, "row", lambda i: (i, i ^ 1))
     x_out = lambda i: (i, i + 2 if i % 2 else i - 2)
     x_in = lambda i: (i, i - 2 if i % 2 else i + 2)

time: 111 us -> 112 us (level)
    ppermute x12, waiting for transfers between devices: 10.7 us -> 11.9 us  [shifted(): lax.ppermute(block, axis, [(i, j) for i, j in map(pairs, range(count)) if...]
    ppermute x1, waiting for transfers between devices: 14.2 us -> 13 us  [body(): crossed = lax.ppermute(raw_late, ('row', 'col'), relay_off_pairs())]
  transfers between devices with their start and end apart: 15 -> 15, of which waited for: 5 -> 5; matrix products, arithmetic and copies ran while one was open for 0% -> 0% of each run, Pallas kernels for 25% -> 26%
where the time goes in v1:
time: 112 us
  waiting for transfers between devices  42.6 us (38%)
  starting transfers between devices  33.9 us (30%)
  Pallas kernels  33 us (29%)
  local copies, waits for them, and re-layouts  1.69 us (2%)
    ppermute x12, starting transfers between devices, shifted(): lax.ppermute(block, axis, [(i, j) for i, j in map(pairs, range(count)) if...  20.9 us
    ppermute x2, waiting for transfers between devices, body(): relayed.append(lax.ppermute(passed, ('row', 'col'), relay_off_pairs()))  17.7 us
    pallas_call x6, Pallas kernels, block_part(): pl.pallas_call(functools.partial(block_kernel, mode, lane), in_specs=[SCA...  13.7 us
    ppermute x1, waiting for transfers between devices, body(): crossed = lax.ppermute(raw_late, ('row', 'col'), relay_off_pairs())  13 us
    ppermute x12, waiting for transfers between devices, shifted(): lax.ppermute(block, axis, [(i, j) for i, j in map(pairs, range(count)) if...  11.9 us
    pallas_call x3, Pallas kernels, call(): pl.pallas_call(functools.partial(product_kernel, [(kind, lane) for _, kin...  8.89 us
    ppermute x2, starting transfers between devices, body(): relayed.append(lax.ppermute(passed, ('row', 'col'), relay_off_pairs()))  7.71 us
    ppermute x1, starting transfers between devices, body(): crossed = lax.ppermute(raw_late, ('row', 'col'), relay_off_pairs())  5.33 us
  transfers between devices with their start and end apart: 15, of which 5 were waited for; matrix products, arithmetic and copies ran while one was open for 0% of the time, Pallas kernels for 26%

profile of v1, /device:TPU:35, one launch (start us, length us, event | category | flops | bytes accessed | tf_op | source)
XLA Modules:
  0.0 111.5 jit_solution(2920373934377257305)
XLA Ops:
  0.0 0.0 copy-start
  0.0 1.7 %copy-done = f32[1536,384]{1,0:T(8,128)S(1)} copy-done((f32[1536,384]{1,0:T(8,128)S(1)}, f32[1536,384]{1,0:T(8,128)}, u32[]{:S(2)}) %copy-start) | copy-done | bytes 2359320
  1.7 0.0 copy-start.1
  1.7 0.1 shard_map.57
  1.8 0.0 copy-start.3
  1.8 0.0 copy-start.4
  1.8 0.0 copy-start.5
  1.8 5.3 %collective-permute-start.6 = (f32[1536,128]{1,0:T(8,128)S(1)}, f32[1536,128]{1,0:T(8,128)S(1)}, u32[]{:S(2)}, u32[]{:S(2)}) collective-permute-start(f32[1536,128]{1,0:T(8,128)S(1)} %get-tuple-element.21), channel_id=1, source_target_pairs={{1,34},{2,33},{3,36},{4,35},{5,38},{6,37},{7,40},{8,39},{9,42},{10... | collective-permute-start | bytes 2359304 | tf_op jit(solution)/shard_map/ppermute | solution.py:307
  7.2 1.1 %shard_map.62 = f32[1536,128]{1,0:T(8,128)S(1)} custom-call(s32[1]{0:T(128)} %bitcast.spots, f32[1536,384]{1,0:T(8,128)} %field.15), custom_call_target="tpu_custom_call" | custom-call | bytes 4194304 | tf_op jit(solution)/shard_map/pallas_call | solution.py:287
  8.3 0.1 collective-permute-start.11
  8.4 0.0 copy-done.1
  8.4 0.1 shard_map.55
  8.5 1.5 %collective-permute-start.4 = (f32[1536,128]{1,0:T(8,128)S(1)}, f32[1536,128]{1,0:T(8,128)S(1)}, u32[]{:S(2)}, u32[]{:S(2)}) collective-permute-start(f32[1536,128]{1,0:T(8,128)S(1)} %get-tuple-element.19), channel_id=1, source_target_pairs={{0,32},{32,0},{64,96},{96,64},{128,160},{160,128},{192,224},{224,1... | collective-permute-start | bytes 2359304 | tf_op jit(solution)/shard_map/ppermute | solution.py:250
  10.1 2.2 %collective-permute-start.3 = (f32[384,256]{1,0:T(8,128)S(1)}, f32[384,256]{1,0:T(8,128)S(1)}, u32[]{:S(2)}, u32[]{:S(2)}) collective-permute-start(f32[384,256]{1,0:T(8,128)S(1)} %get-tuple-element.18), channel_id=1, source_target_pairs={{32,96},{64,0},{96,160},{128,64},{160,224},{192,128},{33,97},{65,1... | collective-permute-start | bytes 1179656 | tf_op jit(solution)/shard_map/ppermute | solution.py:250
  12.2 13.0 %collective-permute-done.6.field.other = f32[1536,128]{1,0:T(8,128)S(1)} collective-permute-done((f32[1536,128]{1,0:T(8,128)S(1)}, f32[1536,128]{1,0:T(8,128)S(1)}, u32[]{:S(2)}, u32[]{:S(2)}) %collective-permute-start.6) | collective-permute-done | bytes 786464 | tf_op jit(solution)/shard_map/ppermute | solution.py:307
  25.2 0.2 collective-permute-start.8
  25.4 0.0 copy-done.3
  25.4 0.0 copy-done.4
  25.4 0.0 copy-done.5
  25.4 4.5 %weights.1.wide = f32[6,3840,128]{2,1,0:T(8,128)S(1)} custom-call(s32[1]{0:T(128)} %bitcast.spots, s32[96,128]{1,0:T(8,128)S(1)} %bitcast.4, s32[96,128]{1,0:T(8,128)S(1)} %bitcast.6, s32[96,128]{1,0:T(8,128)S(1)} %bitcast.8), custom_call_target="tpu_custom_call" | custom-call | bytes 16777216 | tf_op jit(solution)/shard_map/weights/pallas_call | solution.py:333
  29.9 0.0 collective-permute-done.3.far
  30.0 0.0 collective-permute-done.11.other
  30.0 2.3 %shard_map.63 = (f32[1536,128]{1,0:T(8,128)S(1)}, f32[384,128]{1,0:T(8,128)S(1)}) custom-call(s32[1]{0:T(128)} %bitcast.spots, f32[6,3840,128]{2,1,0:T(8,128)S(1)} %weights.1.wide, f32[384,256]{1,0:T(8,128)S(1)} %collective-permute-done.3.far, f32[1536,384]{1,0:T(8,128)S(1)} %copy-done.1, f32[1536,128]{1,0:T(8,128)S(1)} %collective-permute-done.11.other), custom_call_target="tpu_custom_call" | custom-call | flops 14155776 | bytes 2359296 | tf_op jit(solution)/shard_map/pallas_call | solution.py:346
  32.3 3.1 %collective-permute-start.13 = (f32[384,128]{1,0:T(8,128)S(1)}, f32[384,128]{1,0:T(8,128)S(1)}, u32[]{:S(2)}, u32[]{:S(2)}) collective-permute-start(f32[384,128]{1,0:T(8,128)S(1)} %get-tuple-element.26), channel_id=1, source_target_pairs={{0,64},{64,128},{96,32},{128,192},{160,96},{224,160},{1,65},{65,12... | collective-permute-start | bytes 589832 | tf_op jit(solution)/shard_map/ppermute | solution.py:250
  35.4 9.4 %collective-permute-done.4.other = f32[1536,128]{1,0:T(8,128)S(1)} collective-permute-done((f32[1536,128]{1,0:T(8,128)S(1)}, f32[1536,128]{1,0:T(8,128)S(1)}, u32[]{:S(2)}, u32[]{:S(2)}) %collective-permute-start.4) | collective-permute-done | bytes 786464 | tf_op jit(solution)/shard_map/ppermute | solution.py:250
  44.8 2.3 %shard_map.58 = (f32[1536,128]{1,0:T(8,128)S(1)}, f32[384,128]{1,0:T(8,128)S(1)}) custom-call(s32[1]{0:T(128)} %bitcast.spots, f32[6,3840,128]{2,1,0:T(8,128)S(1)} %weights.1.wide, f32[384,256]{1,0:T(8,128)S(1)} %collective-permute-done.3.far, f32[1536,384]{1,0:T(8,128)S(1)} %copy-done.1, f32[1536,128]{1,0:T(8,128)S(1)} %collective-permute-done.4.other), custom_call_target="tpu_custom_call" | custom-call | flops 14155776 | bytes 2359296 | tf_op jit(solution)/shard_map/pallas_call | solution.py:346
  47.1 3.1 %collective-permute-start.9 = (f32[384,128]{1,0:T(8,128)S(1)}, f32[384,128]{1,0:T(8,128)S(1)}, u32[]{:S(2)}, u32[]{:S(2)}) collective-permute-start(f32[384,128]{1,0:T(8,128)S(1)} %get-tuple-element.24), channel_id=1, source_target_pairs={{0,64},{64,128},{96,32},{128,192},{160,96},{224,160},{1,65},{65,12... | collective-permute-start | bytes 589832 | tf_op jit(solution)/shard_map/ppermute | solution.py:250
  50.2 1.9 %collective-permute-start = (f32[384,128]{1,0:T(8,128)S(1)}, f32[384,128]{1,0:T(8,128)S(1)}, u32[]{:S(2)}, u32[]{:S(2)}) collective-permute-start(f32[384,128]{1,0:T(8,128)S(1)} %get-tuple-element.16), channel_id=1, source_target_pairs={{0,32},{32,64},{64,96},{96,128},{128,160},{160,192},{192,224},{1,3... | collective-permute-start | bytes 589832 | tf_op jit(solution)/shard_map/ppermute | solution.py:250
  52.2 4.3 %collective-permute-start.1 = (f32[384,128]{1,0:T(8,128)S(1)}, f32[384,128]{1,0:T(8,128)S(1)}, u32[]{:S(2)}, u32[]{:S(2)}) collective-permute-start(f32[384,128]{1,0:T(8,128)S(1)} %get-tuple-element.17), channel_id=1, source_target_pairs={{32,0},{64,32},{96,64},{128,96},{160,128},{192,160},{224,192},{33,... | collective-permute-start | bytes 589832 | tf_op jit(solution)/shard_map/ppermute | solution.py:250
  56.4 0.0 collective-permute-done.13.far
  56.4 2.3 %shard_map.64.refs_0_ = f32[1536,128]{1,0:T(8,128)S(1)} custom-call(s32[1]{0:T(128)} %bitcast.spots, f32[6,3840,128]{2,1,0:T(8,128)S(1)} %weights.1.wide, f32[384,128]{1,0:T(8,128)S(1)} %collective-permute-done.13.far, f32[1536,384]{1,0:T(8,128)S(1)} %copy-done.1, f32[1536,128]{1,0:T(8,128)S(1)} %collective-permute-done.11.other), custom_call_target="tpu_custom_call" | custom-call | flops 14155776 | bytes 2359296 | tf_op jit(solution)/shard_map/pallas_call | solution.py:346
  58.7 1.0 collective-permute-start.14
  59.7 0.2 shard_map.59
  60.0 0.0 collective-permute-done.9.far
  60.0 2.8 %collective-permute-start.7 = (f32[384,128]{1,0:T(8,128)S(1)}, f32[384,128]{1,0:T(8,128)S(1)}, u32[]{:S(2)}, u32[]{:S(2)}) collective-permute-start(f32[384,128]{1,0:T(8,128)S(1)} %shard_map.59), channel_id=1, source_target_pairs={{0,64},{64,128},{96,32},{128,192},{160,96},{224,160},{1,65},{65,12... | collective-permute-start | bytes 589832 | tf_op jit(solution)/shard_map/ppermute | solution.py:250
  62.8 2.3 %shard_map.61.refs_0_ = f32[1536,128]{1,0:T(8,128)S(1)} custom-call(s32[1]{0:T(128)} %bitcast.spots, f32[6,3840,128]{2,1,0:T(8,128)S(1)} %weights.1.wide, f32[384,128]{1,0:T(8,128)S(1)} %collective-permute-done.9.far, f32[1536,384]{1,0:T(8,128)S(1)} %copy-done.1, f32[1536,128]{1,0:T(8,128)S(1)} %collective-permute-done.4.other), custom_call_target="tpu_custom_call" | custom-call | flops 14155776 | bytes 2359296 | tf_op jit(solution)/shard_map/pallas_call | solution.py:346
  65.1 2.5 %collective-permute-done.far = f32[384,128]{1,0:T(8,128)S(1)} collective-permute-done((f32[384,128]{1,0:T(8,128)S(1)}, f32[384,128]{1,0:T(8,128)S(1)}, u32[]{:S(2)}, u32[]{:S(2)}) %collective-permute-start) | collective-permute-done | bytes 196640 | tf_op jit(solution)/shard_map/ppermute | solution.py:250
  67.6 4.6 %collective-permute-start.12 = (f32[1536,128]{1,0:T(8,128)S(1)}, f32[1536,128]{1,0:T(8,128)S(1)}, u32[]{:S(2)}, u32[]{:S(2)}) collective-permute-start(f32[1536,128]{1,0:T(8,128)S(1)} %get-tuple-element.25), channel_id=1, source_target_pairs={{1,34},{2,33},{3,36},{4,35},{5,38},{6,37},{7,40},{8,39},{9,42},{10... | collective-permute-start | bytes 2359304 | tf_op jit(solution)/shard_map/ppermute | solution.py:374
  72.1 0.0 collective-permute-done.1.other
  72.2 0.2 collective-permute-start.10
  72.3 2.3 %shard_map.56.refs_0_ = f32[1536,128]{1,0:T(8,128)S(1)} custom-call(s32[1]{0:T(128)} %bitcast.spots, f32[6,3840,128]{2,1,0:T(8,128)S(1)} %weights.1.wide, f32[384,128]{1,0:T(8,128)S(1)} %collective-permute-done.far, f32[1536,384]{1,0:T(8,128)S(1)} %copy-done.1, f32[384,128]{1,0:T(8,128)S(1)} %collective-permute-done.1.other), custom_call_target="tpu_custom_call" | custom-call | flops 14155776 | bytes 2359296 | tf_op jit(solution)/shard_map/pallas_call | solution.py:346
  74.6 0.0 collective-permute-done.7.far
  74.6 0.5 collective-permute-start.2
  75.1 0.0 collective-permute-done.8.field
  75.1 3.2 %collective-permute-start.5 = (f32[1536,128]{1,0:T(8,128)S(1)}, f32[1536,128]{1,0:T(8,128)S(1)}, u32[]{:S(2)}, u32[]{:S(2)}) collective-permute-start(f32[1536,128]{1,0:T(8,128)S(1)} %get-tuple-element.20), channel_id=1, source_target_pairs={{1,34},{2,33},{3,36},{4,35},{5,38},{6,37},{7,40},{8,39},{9,42},{10... | collective-permute-start | bytes 2359304 | tf_op jit(solution)/shard_map/ppermute | solution.py:374
  78.3 4.3 %spread.1 = (bf16[1152,384]{1,0:T(8,128)(2,1)S(1)}, bf16[1152,384]{1,0:T(8,128)(2,1)S(1)}) custom-call(s32[1]{0:T(128)} %bitcast.spots, s32[96,128]{1,0:T(8,128)S(1)} %bitcast.5, s32[96,128]{1,0:T(8,128)S(1)} %bitcast.7, s32[96,128]{1,0:T(8,128)S(1)} %bitcast.9), custom_call_target="tpu_custom_call" | custom-call | flops 21233664 | bytes 1769472 | tf_op jit(solution)/shard_map/spread/pallas_call | solution.py:316
  82.6 0.0 copy-start.2
  82.6 2.3 %shard_map.60.refs_3_ = f32[1536,128]{1,0:T(8,128)S(1)} custom-call(s32[1]{0:T(128)} %bitcast.spots, f32[6,3840,128]{2,1,0:T(8,128)S(1)} %weights.1.wide, f32[384,128]{1,0:T(8,128)S(1)} %collective-permute-done.7.far, f32[1536,128]{1,0:T(8,128)S(1)} %collective-permute-done.8.field, f32[1536,128]{1,0:T(8,128)S(1)} %collective-permute-done.6.field.other), custom_call_target="tpu_custom_call" | custom-call | flops 14155776 | bytes 2359296 | tf_op jit(solution)/shard_map/pallas_call | solution.py:346
  84.9 0.0 collective-permute-done.14.refs_1_
  84.9 0.0 copy-done.2
  84.9 2.1 %shard_map.65.refs_5_ = f32[1536,384]{1,0:T(8,128)S(1)} custom-call(s32[1]{0:T(128)} %bitcast.spots, f32[1536,128]{1,0:T(8,128)S(1)} %shard_map.64.refs_0_, f32[1536,128]{1,0:T(8,128)S(1)} %collective-permute-done.14.refs_1_, bf16[1152,384]{1,0:T(8,128)(2,1)S(1)} %get-tuple-element.22.refs_2_.refs_3_.refs_4_, ...), custom_call_target="tpu_custom_call" | custom-call | flops 905969664 | bytes 6291456 | tf_op jit(solution)/shard_map/pallas_call | solution.py:359
  87.0 12.0 %collective-permute-done.12.refs_2_ = f32[1536,128]{1,0:T(8,128)S(1)} collective-permute-done((f32[1536,128]{1,0:T(8,128)S(1)}, f32[1536,128]{1,0:T(8,128)S(1)}, u32[]{:S(2)}, u32[]{:S(2)}) %collective-permute-start.12) | collective-permute-done | bytes 786464 | tf_op jit(solution)/shard_map/ppermute | solution.py:374
  98.9 0.0 collective-permute-done.10.refs_1_
  98.9 2.7 %shard_map.66.refs_6_ = f32[1536,384]{1,0:T(8,128)S(1)} custom-call(s32[1]{0:T(128)} %bitcast.spots, f32[1536,128]{1,0:T(8,128)S(1)} %shard_map.61.refs_0_, f32[1536,128]{1,0:T(8,128)S(1)} %collective-permute-done.10.refs_1_, f32[1536,128]{1,0:T(8,128)S(1)} %collective-permute-done.12.refs_2_, ...), custom_call_target="tpu_custom_call" | custom-call | flops 1358954496 | bytes 7077888 | tf_op jit(solution)/shard_map/pallas_call | solution.py:359
  101.6 0.0 collective-permute-done.2.refs_1_
  101.7 5.7 %collective-permute-done.5.refs_2_ = f32[1536,128]{1,0:T(8,128)S(1)} collective-permute-done((f32[1536,128]{1,0:T(8,128)S(1)}, f32[1536,128]{1,0:T(8,128)S(1)}, u32[]{:S(2)}, u32[]{:S(2)}) %collective-permute-start.5) | collective-permute-done | bytes 786464 | tf_op jit(solution)/shard_map/ppermute | solution.py:374
  107.4 4.1 %shard_map.67 = f32[1536,384]{1,0:T(8,128)} custom-call(s32[1]{0:T(128)} %bitcast.spots, f32[1536,128]{1,0:T(8,128)S(1)} %shard_map.56.refs_0_, f32[1536,128]{1,0:T(8,128)S(1)} %collective-permute-done.2.refs_1_, f32[1536,128]{1,0:T(8,128)S(1)} %collective-permute-done.5.refs_2_, f32[1536,128]{1,0:T(8,128)S(1)} %shard_map.60.refs_3_, ...), custom_call_target="tpu_custom_call" | custom-call | flops 1811939328 | bytes 7864320 | tf_op jit(solution)/shard_map/pallas_call | solution.py:359
Async XLA Ops:
  0.0 1.7 %copy-start = (f32[1536,384]{1,0:T(8,128)S(1)}, f32[1536,384]{1,0:T(8,128)}, u32[]{:S(2)}) copy-start(f32[1536,384]{1,0:T(8,128)} %field.15) | copy-start | bytes 7077892
  1.7 6.7 %copy-start.1 = (f32[1536,384]{1,0:T(8,128)S(1)}, f32[1536,384]{1,0:T(8,128)}, u32[]{:S(2)}) copy-start(f32[1536,384]{1,0:T(8,128)} %field.15) | copy-start | bytes 7077892
  1.8 23.6 %copy-start.3 = (s32[12288]{0:T(1024)S(1)}, s32[12288]{0:T(1024)}, u32[]{:S(2)}) copy-start(s32[12288]{0:T(1024)} %param.7) | copy-start | bytes 147460
  1.8 23.6 %copy-start.4 = (s32[12288]{0:T(1024)S(1)}, s32[12288]{0:T(1024)}, u32[]{:S(2)}) copy-start(s32[12288]{0:T(1024)} %param.8) | copy-start | bytes 147460
  1.8 23.6 %copy-start.5 = (s32[12288]{0:T(1024)S(1)}, s32[12288]{0:T(1024)}, u32[]{:S(2)}) copy-start(s32[12288]{0:T(1024)} %param.9) | copy-start | bytes 147460
  1.8 23.4 %collective-permute-start.6 = (f32[1536,128]{1,0:T(8,128)S(1)}, f32[1536,128]{1,0:T(8,128)S(1)}, u32[]{:S(2)}, u32[]{:S(2)}) collective-permute-start(f32[1536,128]{1,0:T(8,128)S(1)} %get-tuple-element.21), channel_id=1, source_target_pairs={{1,34},{2,33},{3,36},{4,35},{5,38},{6,37},{7,40},{8,39},{9,42},{10... | collective-permute-start | bytes 2359304 | tf_op jit(solution)/shard_map/ppermute | solution.py:307
  8.3 21.7 %collective-permute-start.11 = (f32[1536,128]{1,0:T(8,128)S(1)}, f32[1536,128]{1,0:T(8,128)S(1)}, u32[]{:S(2)}, u32[]{:S(2)}) collective-permute-start(f32[1536,128]{1,0:T(8,128)S(1)} %shard_map.62), channel_id=1, source_target_pairs={{0,32},{32,0},{64,96},{96,64},{128,160},{160,128},{192,224},{224,1... | collective-permute-start | bytes 2359304 | tf_op jit(solution)/shard_map/ppermute | solution.py:250
  8.5 36.3 %collective-permute-start.4 = (f32[1536,128]{1,0:T(8,128)S(1)}, f32[1536,128]{1,0:T(8,128)S(1)}, u32[]{:S(2)}, u32[]{:S(2)}) collective-permute-start(f32[1536,128]{1,0:T(8,128)S(1)} %get-tuple-element.19), channel_id=1, source_target_pairs={{0,32},{32,0},{64,96},{96,64},{128,160},{160,128},{192,224},{224,1... | collective-permute-start | bytes 2359304 | tf_op jit(solution)/shard_map/ppermute | solution.py:250
  10.1 19.9 %collective-permute-start.3 = (f32[384,256]{1,0:T(8,128)S(1)}, f32[384,256]{1,0:T(8,128)S(1)}, u32[]{:S(2)}, u32[]{:S(2)}) collective-permute-start(f32[384,256]{1,0:T(8,128)S(1)} %get-tuple-element.18), channel_id=1, source_target_pairs={{32,96},{64,0},{96,160},{128,64},{160,224},{192,128},{33,97},{65,1... | collective-permute-start | bytes 1179656 | tf_op jit(solution)/shard_map/ppermute | solution.py:250
  25.2 49.9 %collective-permute-start.8 = (f32[1536,128]{1,0:T(8,128)S(1)}, f32[1536,128]{1,0:T(8,128)S(1)}, u32[]{:S(2)}, u32[]{:S(2)}) collective-permute-start(f32[1536,128]{1,0:T(8,128)S(1)} %collective-permute-done.6.field.other), channel_id=1, source_target_pairs={{0,32},{32,0},{64,96},{96,64},{128,160},{160,128},{192,224},{224,1... | collective-permute-start | bytes 2359304 | tf_op jit(solution)/shard_map/ppermute | solution.py:250
  32.3 24.2 %collective-permute-start.13 = (f32[384,128]{1,0:T(8,128)S(1)}, f32[384,128]{1,0:T(8,128)S(1)}, u32[]{:S(2)}, u32[]{:S(2)}) collective-permute-start(f32[384,128]{1,0:T(8,128)S(1)} %get-tuple-element.26), channel_id=1, source_target_pairs={{0,64},{64,128},{96,32},{128,192},{160,96},{224,160},{1,65},{65,12... | collective-permute-start | bytes 589832 | tf_op jit(solution)/shard_map/ppermute | solution.py:250
  47.1 12.9 %collective-permute-start.9 = (f32[384,128]{1,0:T(8,128)S(1)}, f32[384,128]{1,0:T(8,128)S(1)}, u32[]{:S(2)}, u32[]{:S(2)}) collective-permute-start(f32[384,128]{1,0:T(8,128)S(1)} %get-tuple-element.24), channel_id=1, source_target_pairs={{0,64},{64,128},{96,32},{128,192},{160,96},{224,160},{1,65},{65,12... | collective-permute-start | bytes 589832 | tf_op jit(solution)/shard_map/ppermute | solution.py:250
  50.2 17.4 %collective-permute-start = (f32[384,128]{1,0:T(8,128)S(1)}, f32[384,128]{1,0:T(8,128)S(1)}, u32[]{:S(2)}, u32[]{:S(2)}) collective-permute-start(f32[384,128]{1,0:T(8,128)S(1)} %get-tuple-element.16), channel_id=1, source_target_pairs={{0,32},{32,64},{64,96},{96,128},{128,160},{160,192},{192,224},{1,3... | collective-permute-start | bytes 589832 | tf_op jit(solution)/shard_map/ppermute | solution.py:250
  52.2 20.0 %collective-permute-start.1 = (f32[384,128]{1,0:T(8,128)S(1)}, f32[384,128]{1,0:T(8,128)S(1)}, u32[]{:S(2)}, u32[]{:S(2)}) collective-permute-start(f32[384,128]{1,0:T(8,128)S(1)} %get-tuple-element.17), channel_id=1, source_target_pairs={{32,0},{64,32},{96,64},{128,96},{160,128},{192,160},{224,192},{33,... | collective-permute-start | bytes 589832 | tf_op jit(solution)/shard_map/ppermute | solution.py:250
  58.7 26.2 %collective-permute-start.14 = (f32[1536,128]{1,0:T(8,128)S(1)}, f32[1536,128]{1,0:T(8,128)S(1)}, u32[]{:S(2)}, u32[]{:S(2)}) collective-permute-start(f32[1536,128]{1,0:T(8,128)S(1)} %shard_map.64.refs_0_), channel_id=1, source_target_pairs={{0,1},{1,0},{2,3},{3,2},{4,5},{5,4},{6,7},{7,6},{8,9},{9,8},{10,11... | collective-permute-start | bytes 2359304 | tf_op jit(solution)/shard_map/ppermute | solution.py:250
  60.0 14.6 %collective-permute-start.7 = (f32[384,128]{1,0:T(8,128)S(1)}, f32[384,128]{1,0:T(8,128)S(1)}, u32[]{:S(2)}, u32[]{:S(2)}) collective-permute-start(f32[384,128]{1,0:T(8,128)S(1)} %shard_map.59), channel_id=1, source_target_pairs={{0,64},{64,128},{96,32},{128,192},{160,96},{224,160},{1,65},{65,12... | collective-permute-start | bytes 589832 | tf_op jit(solution)/shard_map/ppermute | solution.py:250
  67.6 31.4 %collective-permute-start.12 = (f32[1536,128]{1,0:T(8,128)S(1)}, f32[1536,128]{1,0:T(8,128)S(1)}, u32[]{:S(2)}, u32[]{:S(2)}) collective-permute-start(f32[1536,128]{1,0:T(8,128)S(1)} %get-tuple-element.25), channel_id=1, source_target_pairs={{1,34},{2,33},{3,36},{4,35},{5,38},{6,37},{7,40},{8,39},{9,42},{10... | collective-permute-start | bytes 2359304 | tf_op jit(solution)/shard_map/ppermute | solution.py:374
  72.2 26.8 %collective-permute-start.10 = (f32[1536,128]{1,0:T(8,128)S(1)}, f32[1536,128]{1,0:T(8,128)S(1)}, u32[]{:S(2)}, u32[]{:S(2)}) collective-permute-start(f32[1536,128]{1,0:T(8,128)S(1)} %shard_map.61.refs_0_), channel_id=1, source_target_pairs={{0,1},{1,0},{2,3},{3,2},{4,5},{5,4},{6,7},{7,6},{8,9},{9,8},{10,11... | collective-permute-start | bytes 2359304 | tf_op jit(solution)/shard_map/ppermute | solution.py:250
  74.6 27.0 %collective-permute-start.2 = (f32[1536,128]{1,0:T(8,128)S(1)}, f32[1536,128]{1,0:T(8,128)S(1)}, u32[]{:S(2)}, u32[]{:S(2)}) collective-permute-start(f32[1536,128]{1,0:T(8,128)S(1)} %shard_map.56.refs_0_), channel_id=1, source_target_pairs={{0,1},{1,0},{2,3},{3,2},{4,5},{5,4},{6,7},{7,6},{8,9},{9,8},{10,11... | collective-permute-start | bytes 2359304 | tf_op jit(solution)/shard_map/ppermute | solution.py:250
  75.1 32.2 %collective-permute-start.5 = (f32[1536,128]{1,0:T(8,128)S(1)}, f32[1536,128]{1,0:T(8,128)S(1)}, u32[]{:S(2)}, u32[]{:S(2)}) collective-permute-start(f32[1536,128]{1,0:T(8,128)S(1)} %get-tuple-element.20), channel_id=1, source_target_pairs={{1,34},{2,33},{3,36},{4,35},{5,38},{6,37},{7,40},{8,39},{9,42},{10... | collective-permute-start | bytes 2359304 | tf_op jit(solution)/shard_map/ppermute | solution.py:374
  82.6 2.3 %copy-start.2 = (f32[1536,384]{1,0:T(8,128)S(1)}, f32[1536,384]{1,0:T(8,128)}, u32[]{:S(2)}) copy-start(f32[1536,384]{1,0:T(8,128)} %refs_4_.1) | copy-start | bytes 7077892
